TPU v7x, 32 devices: a whole 2x2x4 slice. The times are simulated.
32 devices in a mesh: group: 2 (over y), replica: 16 (over z, x, core).
Axes of the slice: x: 2, y: 2, z: 4, core: 2. Of those that a mesh axis runs over, the one named last changes fastest.
Arguments:
- tokens: bfloat16 [32, 144, 896], P(('group', 'replica')), may hold values from -6 to 6
- segments: int32 [32, 144], P(('group', 'replica')), may hold values from 0 to 35, never falling along the last dimension, each value on 1 to 72 neighbouring positions
- norm1_gain: bfloat16 [896], P('group'), may hold values from 0.5 to 1.5
- qkv_weight: bfloat16 [896, 1152], P('group'), may hold values from -0.1875 to 0.1875
- qkv_bias: bfloat16 [1152], P('group'), may hold values from -2.5 to 2.5
- out_weight: bfloat16 [896, 896], P('group'), may hold values from -0.375 to 0.375
- norm2_gain: bfloat16 [896], P('group'), may hold values from 0.5 to 1.5
- gate_weight: bfloat16 [896, 4864], P(None, 'group'), may hold values from -0.1875 to 0.1875
- up_weight: bfloat16 [896, 4864], P(None, 'group'), may hold values from -0.1875 to 0.1875
- down_weight: bfloat16 [4864, 896], P('group'), may hold values from -0.078125 to 0.078125
- cotangent: bfloat16 [32, 144, 896], P(('group', 'replica')), may hold values from -6 to 6
Outputs:
- result: float32 [32, 144, 896], P(('group', 'replica'))
- back_tokens: float32 [32, 144, 896], P(('group', 'replica'))
- grad_norm1: float32 [896], P('group')
- grad_qkv: float32 [896, 1152], P('group')
- grad_bias: float32 [1152], P('group')
- grad_out: float32 [896, 896], P('group')
- grad_norm2: float32 [896], P('group')
- grad_gate: float32 [896, 4864], P(None, 'group')
- grad_up: float32 [896, 4864], P(None, 'group')
- grad_down: float32 [4864, 896], P('group')
Inputs may be any that keep to these rules, and one draw needn't show every extreme that they name: `segments`: segment ids never fall along a sequence.
All inputs are finite; a program needn't handle non-finite values.
Results may differ from a plain program's by a relative error of at most 0.023.
Values may be sent and summed in bfloat16 or wider, within the bound.
A program may use at most 192 MiB of HBM per device.

v0:
```python
import jax
import jax.numpy as jnp
from jax import lax
from jax.sharding import PartitionSpec as P

H = 14
KV = 2
HD = 64
EPSILON = 1e-06
ROPE_BASE = 1000000.0
NEG_LARGE = -1e30


def doc_layout(segments, head_dim):
    length = segments.shape[1]
    places = jnp.arange(length, dtype=jnp.int32)
    same_doc = segments[:, :, None] == segments[:, None, :]
    earlier = places[None, None, :] < places[None, :, None]
    positions = jnp.sum(jnp.where(same_doc & earlier, 1.0, 0.0).astype(jnp.float32), axis=2)
    allowed = jnp.where(same_doc & (places[None, None, :] <= places[None, :, None]), 1, 0).astype(
        jnp.int32
    )
    half_dim = head_dim // 2
    frequency = ROPE_BASE ** (-2.0 * jnp.arange(half_dim, dtype=jnp.float32) / head_dim)
    angles = positions[:, :, None] * frequency[None, None, :]
    return (allowed, jnp.cos(angles)[:, :, None, :], jnp.sin(angles)[:, :, None, :])


def rotate(values, cosine, sine):
    half_dim = values.shape[-1] // 2
    front_half = values[..., :half_dim]
    back_half = values[..., half_dim:]
    return jnp.concatenate(
        [front_half * cosine - back_half * sine, back_half * cosine + front_half * sine], axis=-1
    )


def unrotate(gradients, cosine, sine):
    half_dim = gradients.shape[-1] // 2
    front_half = gradients[..., :half_dim]
    back_half = gradients[..., half_dim:]
    return jnp.concatenate(
        [front_half * cosine + back_half * sine, back_half * cosine - front_half * sine], axis=-1
    )


def inverse_rms(hidden):
    return lax.rsqrt(jnp.mean(hidden * hidden, axis=-1, keepdims=True) + EPSILON)


def norm_backward(hidden, inv_rms, gain_f, back_normed):
    weighted = back_normed * gain_f
    inner = jnp.mean(weighted * hidden, axis=-1, keepdims=True)
    back_hidden = inv_rms * weighted - hidden * (inv_rms * inv_rms * inv_rms) * inner
    back_gain = jnp.sum(back_normed * hidden * inv_rms, axis=0)
    return (back_hidden, back_gain)


def matmul(left, right):
    return jnp.dot(left, right, preferred_element_type=jnp.float32)


def outer_sum(left, right):
    return lax.dot_general(
        left, right, (((0,), (0,)), ((), ())), preferred_element_type=jnp.float32
    )


def times_transposed(left, right):
    return lax.dot_general(
        left, right, (((1,), (1,)), ((), ())), preferred_element_type=jnp.float32
    )


def score_block(query_b, keys_b, allowed, score_scale):
    scores = (
        jnp.einsum("sqkgd,spkd->skgqp", query_b, keys_b, preferred_element_type=jnp.float32)
        * score_scale
    )
    return jnp.where(allowed[:, None, None, :, :] > 0, scores, NEG_LARGE)


def on_device(
    tokens,
    segments,
    norm1_gain,
    qkv_weight,
    qkv_bias,
    out_weight,
    norm2_gain,
    gate_weight,
    up_weight,
    down_weight,
    cotangent,
):
    sequences, length, model_width = tokens.shape
    row_count = sequences * length
    q_width = H * HD
    kv_width = KV * HD
    groups = H // KV
    score_scale = HD ** (-0.5)
    gain1_b, w_qkv, b_qkv, w_out, gain2_b = (
        lax.all_gather(norm1_gain, "group", axis=0, tiled=True),
        lax.all_gather(qkv_weight, "group", axis=0, tiled=True),
        lax.all_gather(qkv_bias, "group", axis=0, tiled=True),
        lax.all_gather(out_weight, "group", axis=0, tiled=True),
        lax.all_gather(norm2_gain, "group", axis=0, tiled=True),
    )
    allowed, cosine, sine = doc_layout(segments, HD)
    resid_in = tokens.reshape(row_count, model_width).astype(jnp.float32)
    inv_rms1 = inverse_rms(resid_in)
    gain1 = gain1_b.astype(jnp.float32)
    normed1 = (resid_in * inv_rms1 * gain1).astype(jnp.bfloat16)
    projected = matmul(normed1, w_qkv) + b_qkv.astype(jnp.float32)
    query = projected[:, :q_width].reshape(sequences, length, H, HD)
    keys_raw = projected[:, q_width : q_width + kv_width].reshape(sequences, length, KV, HD)
    values_raw = projected[:, q_width + kv_width :].reshape(sequences, length, KV, HD)
    query_b = (
        rotate(query, cosine, sine).astype(jnp.bfloat16).reshape(sequences, length, KV, groups, HD)
    )
    keys_b = rotate(keys_raw, cosine, sine).astype(jnp.bfloat16)
    values_b = values_raw.astype(jnp.bfloat16)
    scores = score_block(query_b, keys_b, allowed, score_scale)
    top_score = jnp.max(scores, axis=-1, keepdims=True)
    log_total = top_score + jnp.log(jnp.sum(jnp.exp(scores - top_score), axis=-1, keepdims=True))
    soft_b = jnp.exp(scores - log_total).astype(jnp.bfloat16)
    context = jnp.einsum("skgqp,spkd->sqkgd", soft_b, values_b, preferred_element_type=jnp.float32)
    context_b = context.astype(jnp.bfloat16).reshape(row_count, q_width)
    middle = resid_in + matmul(context_b, w_out)
    inv_rms2 = inverse_rms(middle)
    gain2 = gain2_b.astype(jnp.float32)
    normed2 = (middle * inv_rms2 * gain2).astype(jnp.bfloat16)
    back_rows = cotangent.reshape(row_count, model_width)
    normed_all, back_all = (
        lax.all_gather(normed2, "group", axis=0, tiled=True),
        lax.all_gather(back_rows, "group", axis=0, tiled=True),
    )
    gate_pre = matmul(normed_all, gate_weight)
    up_proj = matmul(normed_all, up_weight)
    sigmoid_gate = jax.nn.sigmoid(gate_pre)
    silu_gate = gate_pre * sigmoid_gate
    activ_b = (silu_gate * up_proj).astype(jnp.bfloat16)
    result = middle + lax.psum_scatter(
        matmul(activ_b, down_weight).astype(jnp.bfloat16), "group", scatter_dimension=0, tiled=True
    ).astype(jnp.float32)
    back_activ = times_transposed(back_all, down_weight)
    back_gate = (
        back_activ * up_proj * sigmoid_gate * (1.0 + gate_pre * (1.0 - sigmoid_gate))
    ).astype(jnp.bfloat16)
    back_up = (back_activ * silu_gate).astype(jnp.bfloat16)
    grad_down = outer_sum(activ_b, back_all)
    grad_gate = outer_sum(normed_all, back_gate)
    grad_up = outer_sum(normed_all, back_up)
    local_normed = times_transposed(back_gate, gate_weight) + times_transposed(back_up, up_weight)
    back_normed2 = lax.psum_scatter(
        local_normed.astype(jnp.bfloat16), "group", scatter_dimension=0, tiled=True
    ).astype(jnp.float32)
    gain1_b, w_qkv, b_qkv, w_out, gain2_b = (
        lax.all_gather(norm1_gain, "group", axis=0, tiled=True),
        lax.all_gather(qkv_weight, "group", axis=0, tiled=True),
        lax.all_gather(qkv_bias, "group", axis=0, tiled=True),
        lax.all_gather(out_weight, "group", axis=0, tiled=True),
        lax.all_gather(norm2_gain, "group", axis=0, tiled=True),
    )
    gain1 = gain1_b.astype(jnp.float32)
    gain2 = gain2_b.astype(jnp.float32)
    back_norm2, grad_norm2_part = norm_backward(middle, inv_rms2, gain2, back_normed2)
    back_middle = back_rows.astype(jnp.float32) + back_norm2
    back_middle_b = back_middle.astype(jnp.bfloat16)
    grad_out_part = outer_sum(context_b, back_middle_b)
    back_context = times_transposed(back_middle_b, w_out).astype(jnp.bfloat16)
    back_context = back_context.reshape(sequences, length, KV, groups, HD)
    soft = jnp.exp(score_block(query_b, keys_b, allowed, score_scale) - log_total)
    soft_again = soft.astype(jnp.bfloat16)
    back_values = jnp.einsum(
        "skgqp,sqkgd->spkd", soft_again, back_context, preferred_element_type=jnp.float32
    )
    back_soft = jnp.einsum(
        "sqkgd,spkd->skgqp", back_context, values_b, preferred_element_type=jnp.float32
    )
    row_dot = jnp.sum(soft * back_soft, axis=-1, keepdims=True)
    back_scores = (soft * (back_soft - row_dot) * score_scale).astype(jnp.bfloat16)
    back_query = jnp.einsum(
        "skgqp,spkd->sqkgd", back_scores, keys_b, preferred_element_type=jnp.float32
    )
    back_keys = jnp.einsum(
        "skgqp,sqkgd->spkd", back_scores, query_b, preferred_element_type=jnp.float32
    )
    back_query = unrotate(back_query.reshape(sequences, length, H, HD), cosine, sine)
    back_keys = unrotate(back_keys, cosine, sine)
    back_proj = jnp.concatenate(
        [
            back_query.reshape(row_count, q_width),
            back_keys.reshape(row_count, kv_width),
            back_values.reshape(row_count, kv_width),
        ],
        axis=1,
    )
    grad_bias_part = jnp.sum(back_proj, axis=0)
    back_proj_b = back_proj.astype(jnp.bfloat16)
    grad_qkv_part = outer_sum(normed1, back_proj_b)
    back_normed1 = times_transposed(back_proj_b, w_qkv)
    back_norm1, grad_norm1_part = norm_backward(resid_in, inv_rms1, gain1, back_normed1)
    back_tokens = back_middle + back_norm1
    grad_norm1, grad_qkv, grad_bias, grad_out, grad_norm2 = (
        lax.psum_scatter(
            grad_norm1_part.astype(jnp.bfloat16), "group", scatter_dimension=0, tiled=True
        ).astype(jnp.float32),
        lax.psum_scatter(
            grad_qkv_part.astype(jnp.bfloat16), "group", scatter_dimension=0, tiled=True
        ).astype(jnp.float32),
        lax.psum_scatter(
            grad_bias_part.astype(jnp.bfloat16), "group", scatter_dimension=0, tiled=True
        ).astype(jnp.float32),
        lax.psum_scatter(
            grad_out_part.astype(jnp.bfloat16), "group", scatter_dimension=0, tiled=True
        ).astype(jnp.float32),
        lax.psum_scatter(
            grad_norm2_part.astype(jnp.bfloat16), "group", scatter_dimension=0, tiled=True
        ).astype(jnp.float32),
    )
    grad_norm1, grad_qkv, grad_bias, grad_out, grad_norm2, grad_gate, grad_up, grad_down = (
        lax.psum(grad_norm1.astype(jnp.bfloat16), "replica").astype(jnp.float32),
        lax.psum(grad_qkv.astype(jnp.bfloat16), "replica").astype(jnp.float32),
        lax.psum(grad_bias.astype(jnp.bfloat16), "replica").astype(jnp.float32),
        lax.psum(grad_out.astype(jnp.bfloat16), "replica").astype(jnp.float32),
        lax.psum(grad_norm2.astype(jnp.bfloat16), "replica").astype(jnp.float32),
        lax.psum(grad_gate.astype(jnp.bfloat16), "replica").astype(jnp.float32),
        lax.psum(grad_up.astype(jnp.bfloat16), "replica").astype(jnp.float32),
        lax.psum(grad_down.astype(jnp.bfloat16), "replica").astype(jnp.float32),
    )
    shape_out = (sequences, length, model_width)
    return (
        result.reshape(shape_out),
        back_tokens.reshape(shape_out),
        grad_norm1,
        grad_qkv,
        grad_bias,
        grad_out,
        grad_norm2,
        grad_gate,
        grad_up,
        grad_down,
    )


def solution(mesh):
    in_specs = (
        P(("group", "replica"), None, None),
        P(("group", "replica"), None),
        P("group"),
        P("group", None),
        P("group"),
        P("group", None),
        P("group"),
        P(None, "group"),
        P(None, "group"),
        P("group", None),
        P(("group", "replica"), None, None),
    )
    out_specs = (
        P(("group", "replica"), None, None),
        P(("group", "replica"), None, None),
        P("group"),
        P("group", None),
        P("group"),
        P("group", None),
        P("group"),
        P(None, "group"),
        P(None, "group"),
        P("group", None),
    )
    return jax.shard_map(
        on_device, mesh=mesh, in_specs=in_specs, out_specs=out_specs, check_vma=False
    )
```

profile of v0, /device:TPU:0, one launch (start us, length us, event | category | flops | bytes accessed | tf_op | source)
XLA Modules:
  0.0 505.1 jit_solution(13327327023692084482)
XLA Ops:
  14.7 5.9 %all-reduce.9 = (bf16[1152]{0:T(1024)(128)(2,1)S(1)}, bf16[896]{0:T(1024)(128)(2,1)S(1)}, bf16[896]{0:T(1024)(128)(2,1)S(1)}) all-reduce(bf16[1152]{0:T(1024)(128)(2,1)S(1)} %dynamic-update-slice.1, bf16[896]{0:T(1024)(128)(2,1)S(1)} %dynamic-update-slice, ...), channel_id=1, replica_groups=mesh['group'=2,'replica'=16] {'group'}, use_global_device_ids=true, to_apply=%add.1 | all-reduce | flops 2944 | bytes 11776
  21.0 14.6 %all-gather = bf16[1,288,896]{2,1,0:T(8,128)(2,1)} all-gather(bf16[1,144,896]{2,1,0:T(8,128)(2,1)S(1)} %copy-done.6), channel_id=2, replica_groups=mesh['group'=2,'replica'=16] {'group'}, dimensions={1}, use_global_device_ids=true | all-gather | bytes 774144 | tf_op jit(solution)/shard_map/all_gather | solution.py:136
  35.6 15.0 %all-gather.4.cloned.1.call-done = bf16[896,1152]{1,0:T(8,128)(2,1)} async-done(((bf16[448,1152]{1,0:T(8,128)(2,1)}), bf16[896,1152]{1,0:T(8,128)(2,1)}) %all-gather.4.cloned.1.call-update) | async-done | bytes 2064400 | tf_op jit(solution)/shard_map/all_gather | solution.py:104
  56.6 23.2 %all-gather.6.cloned.1.call-done = bf16[896,896]{1,0:T(8,128)(2,1)} async-done(((bf16[448,896]{1,0:T(8,128)(2,1)}), bf16[896,896]{1,0:T(8,128)(2,1)}) %all-gather.6.cloned.1.call-update) | async-done | bytes 1605648 | tf_op jit(solution)/shard_map/all_gather | solution.py:106
  82.0 8.9 %all_gather.30 = bf16[288,896]{1,0:T(8,128)(2,1)S(1)} all-gather(bf16[144,896]{1,0:T(8,128)(2,1)S(1)} %multiply_convert_fusion.3), channel_id=1, replica_groups=mesh['group'=2,'replica'=16] {'group'}, dimensions={0}, use_global_device_ids=true | all-gather | bytes 774144 | tf_op jit(solution)/shard_map/all_gather | solution.py:135
  91.0 4.1 fusion.53
  96.9 4.0 multiply_convert_fusion
  102.7 2.5 fusion.6
  105.3 5.1 %convolution_convert_fusion.5 = bf16[288,896]{1,0:T(8,128)(2,1)} fusion(bf16[288,2432]{1,0:T(8,128)(2,1)} %get-tuple-element.30, bf16[2432,896]{1,0:T(8,128)(2,1)} %param.20), kind=kOutput, calls=%fused_computation.22 | convolution fusion | flops 1255403520 | bytes 6275072 | tf_op jit(solution)/shard_map/dot_general | solution.py:60
  110.5 9.4 %reduce-scatter.7.cloned.1.call-done = bf16[144,896]{1,0:T(8,128)(2,1)} async-done(((bf16[288,896]{1,0:T(8,128)(2,1)}), bf16[144,896]{1,0:T(8,128)(2,1)}) %reduce-scatter.7.cloned.1.call-update) | async-done | bytes 258064 | tf_op jit(solution)/shard_map/reduce_scatter | solution.py:155
  121.0 16.1 %reduce-scatter.5.cloned.1.call-done = bf16[144,896]{1,0:T(8,128)(2,1)} async-done(((bf16[288,896]{1,0:T(8,128)(2,1)}), bf16[144,896]{1,0:T(8,128)(2,1)}) %reduce-scatter.5.cloned.1.call-update) | async-done | bytes 258064 | tf_op jit(solution)/shard_map/reduce_scatter | solution.py:143
  139.3 3.0 convolution_convert_fusion.4
  142.6 2.7 convolution_convert_fusion.7
  154.9 4.7 convolution_convert_fusion
  159.6 4.6 convolution_convert_fusion.1
  164.2 4.6 convolution_convert_fusion.2
  168.9 34.2 %reduce-scatter.9.cloned.1.call-done = bf16[448,1152]{1,0:T(8,128)(2,1)} async-done(((bf16[896,1152]{1,0:T(8,128)(2,1)}), bf16[448,1152]{1,0:T(8,128)(2,1)}) %reduce-scatter.9.cloned.1.call-update) | async-done | bytes 1032208 | tf_op jit(solution)/shard_map/reduce_scatter | solution.py:209
  206.3 5.0 all-reduce.8
  211.5 33.8 %all-reduce.6 = (bf16[448]{0:T(512)(128)(2,1)S(1)}, bf16[576]{0:T(1024)(128)(2,1)S(1)}, bf16[448]{0:T(512)(128)(2,1)S(1)}) all-reduce(bf16[448]{0:T(512)(128)(2,1)S(1)} %dynamic-slice.4, bf16[576]{0:T(1024)(128)(2,1)S(1)} %dynamic-slice.6, bf16[448]{0:T(512)(128)(2,1)S(1)} %dynamic-slice.8), channel_id=1, replica_groups=mesh['group'=2,'replica'=16] {'replica'}, use_global_device_ids=true, to_apply=%region_12.13 | all-reduce | flops 1472 | bytes 5888 | tf_op jit(solution)/shard_map/psum | solution.py:223
  249.1 232.0 %all-reduce.12.cloned.1.call-done = (bf16[448,1152]{1,0:T(8,128)(2,1)}, bf16[448,896]{1,0:T(8,128)(2,1)}, bf16[896,2432]{1,0:T(8,128)(2,1)}, bf16[896,2432]{1,0:T(8,128)(2,1)}, bf16[2432,896]{1,0:T(8,128)(2,1)}) async-done(((bf16[448,1152]{1,0:T(8,128)(2,1)}, bf16[448,896]{1,0:T(8,128)(2,1)}, bf16[896,2432]{1,0:T(8,128)(2,1)}, bf16[896,2432]{1,0:T(8,128)(2,1)}, bf16[2432,896]{1,0:T(8,128)(2,1)}), ...) | async-done | bytes 14909456 | tf_op jit(solution)/shard_map/psum | solution.py:224
  481.1 2.8 convert_element_type.176
  485.2 4.9 convert_element_type.184
  490.1 4.1 convert_element_type.186
  494.1 4.1 convert_element_type.188
  (180 shorter events, 38.1 us)
Async XLA Ops:
  7.2 6.1 %copy-start.2 = (bf16[1,144,896]{2,1,0:T(8,128)(2,1)S(1)}, bf16[1,144,896]{2,1,0:T(8,128)(2,1)}, u32[]{:S(2)}) copy-start(bf16[1,144,896]{2,1,0:T(8,128)(2,1)} %param.11) | copy-start | bytes 774148
  7.2 6.8 %copy-start.28 = (bf16[448]{0:T(512)(128)(2,1)S(1)}, bf16[448]{0:T(512)(128)(2,1)}, u32[]{:S(2)}) copy-start(bf16[448]{0:T(512)(128)(2,1)} %param.13) | copy-start | bytes 2692
  7.2 7.0 %copy-start.29 = (bf16[448]{0:T(512)(128)(2,1)S(1)}, bf16[448]{0:T(512)(128)(2,1)}, u32[]{:S(2)}) copy-start(bf16[448]{0:T(512)(128)(2,1)} %param.17) | copy-start | bytes 2692
  7.2 7.2 %copy-start.27 = (bf16[576]{0:T(1024)(128)(2,1)S(1)}, bf16[576]{0:T(1024)(128)(2,1)}, u32[]{:S(2)}) copy-start(bf16[576]{0:T(1024)(128)(2,1)} %param.15) | copy-start | bytes 3460
  7.2 13.8 %copy-start.6 = (bf16[1,144,896]{2,1,0:T(8,128)(2,1)S(1)}, bf16[1,144,896]{2,1,0:T(8,128)(2,1)}, u32[]{:S(2)}) copy-start(bf16[1,144,896]{2,1,0:T(8,128)(2,1)} %param.21) | copy-start | bytes 774148
  7.2 43.4 %all-gather.4.cloned.1.call-start = ((), (), s32[]{:S(2)}) async-start(), calls=%async_computation.4 | async-start | bytes 3096576 | tf_op jit(solution)/shard_map/all_gather | solution.py:104
  8.0 71.8 %all-gather.6.cloned.1.call-start = ((), (), s32[]{:S(2)}) async-start(), calls=%async_computation.5 | async-start | bytes 2408448 | tf_op jit(solution)/shard_map/all_gather | solution.py:106
  8.7 111.1 %reduce-scatter.7.cloned.1.call-start = ((), (), s32[]{:S(2)}) async-start(), calls=%async_computation.7 | async-start | bytes 774144 | tf_op jit(solution)/shard_map/reduce_scatter | solution.py:155
  20.8 34.3 %copy-start.16 = (f32[144,32]{0,1:T(8,128)}, f32[144,32]{0,1:T(8,128)S(1)}, u32[]{:S(2)}) copy-start(f32[144,32]{0,1:T(8,128)S(1)} %get-tuple-element.44) | copy-start | bytes 55300
  20.9 32.6 %copy-start.12 = (f32[144,32]{1,0:T(8,128)}, f32[144,32]{1,0:T(8,128)S(1)}, u32[]{:S(2)}) copy-start(f32[144,32]{1,0:T(8,128)S(1)} %copy.77) | copy-start | bytes 55300
  21.0 32.5 %copy-start.14 = (f32[144,32]{1,0:T(8,128)}, f32[144,32]{1,0:T(8,128)S(1)}, u32[]{:S(2)}) copy-start(f32[144,32]{1,0:T(8,128)S(1)} %copy.78) | copy-start | bytes 55300
  56.5 34.4 %copy-start.4 = (bf16[2,64,7,144]{3,1,2,0:T(8,128)(2,1)}, bf16[2,64,7,144]{3,1,2,0:T(8,128)(2,1)S(1)}, u32[]{:S(2)}) copy-start(bf16[2,64,7,144]{3,1,2,0:T(8,128)(2,1)S(1)} %convolution_convert_fusion.6) | copy-start | bytes 774148
  82.0 13.1 %slice-start.4 = ((s8[4358144]{0:T(1024)(128)(4,1)}), s8[4194304]{0:T(1024)(128)(4,1)S(1)}, s32[]{:S(2)}) async-start(s8[4358144]{0:T(1024)(128)(4,1)} %bitcast.142), calls=%async_computation.15 | async-start | bytes 8388608
  91.0 5.9 %slice-start.8 = ((s8[4358144]{0:T(1024)(128)(4,1)}), s8[4194304]{0:T(1024)(128)(4,1)S(1)}, s32[]{:S(2)}) async-start(s8[4358144]{0:T(1024)(128)(4,1)} %bitcast.146), calls=%async_computation.19 | async-start | bytes 8388608
  95.2 7.5 %slice-start.6 = ((s8[4358144]{0:T(1024)(128)(4,1)}), s8[4194304]{0:T(1024)(128)(4,1)S(1)}, s32[]{:S(2)}) async-start(s8[4358144]{0:T(1024)(128)(4,1)} %bitcast.144), calls=%async_computation.17 | async-start | bytes 8388608
  96.9 5.8 %slice-start.7 = ((s8[4358144]{0:T(1024)(128)(4,1)}), s8[163840]{0:T(1024)(128)(4,1)S(1)}, s32[]{:S(2)}) async-start(s8[4358144]{0:T(1024)(128)(4,1)} %bitcast.144), calls=%async_computation.18 | async-start | bytes 327680
  105.2 31.9 %reduce-scatter.5.cloned.1.call-start = ((), (), s32[]{:S(2)}) async-start(), calls=%async_computation.6 | async-start | bytes 774144 | tf_op jit(solution)/shard_map/reduce_scatter | solution.py:143
  110.4 58.5 %reduce-scatter.11.cloned.1.call-start = ((), (), s32[]{:S(2)}) async-start(), calls=%async_computation.9 | async-start | bytes 2408448 | tf_op jit(solution)/shard_map/reduce_scatter | solution.py:215
  142.3 60.8 %reduce-scatter.9.cloned.1.call-start = ((), (), s32[]{:S(2)}) async-start(), calls=%async_computation.8 | async-start | bytes 3096576 | tf_op jit(solution)/shard_map/reduce_scatter | solution.py:209
  154.6 326.5 %all-reduce.12.cloned.1.call-start = ((), (), s32[]{:S(2)}) async-start(), calls=%async_computation.10 | async-start | bytes 29818880 | tf_op jit(solution)/shard_map/psum | solution.py:224
  204.6 42.4 %copy-start.1 = (f32[144,896]{1,0:T(8,128)S(1)}, f32[144,896]{1,0:T(8,128)}, u32[]{:S(2)}) copy-start(f32[144,896]{1,0:T(8,128)} %copy-done) | copy-start | bytes 1548292
  204.6 42.4 %copy-start.26 = (f32[144]{0:T(256)S(1)}, f32[144]{0:T(256)}, u32[]{:S(2)}) copy-start(f32[144]{0:T(256)} %get-tuple-element.45) | copy-start | bytes 1732
  483.9 6.1 %slice-start.2 = ((s8[4358144]{0:T(1024)(128)(4,1)}), s8[4194304]{0:T(1024)(128)(4,1)S(1)}, s32[]{:S(2)}) async-start(s8[4358144]{0:T(1024)(128)(4,1)} %bitcast.125), calls=%async_computation.13 | async-start | bytes 8388608
  485.2 9.0 %slice-start = ((s8[4358144]{0:T(1024)(128)(4,1)}), s8[4194304]{0:T(1024)(128)(4,1)S(1)}, s32[]{:S(2)}) async-start(s8[4358144]{0:T(1024)(128)(4,1)} %bitcast.123), calls=%async_computation.11 | async-start | bytes 8388608
  (28 other events, 67.6 us)
Sparse Core Ops, SparseCore 0:
  9.6 40.9 all-gather.3
  52.2 27.5 all-gather.5
  105.3 14.4 reduce-scatter.6
  122.6 14.4 reduce-scatter.4
  142.4 26.4 reduce-scatter.10
  171.6 31.4 reduce-scatter.8
  209.3 271.7 all-reduce.11
where the time goes:
time: 506 us; the launch traced here: 505 us
  waiting for transfers between devices  332 us (66%)
  blocking collectives  68.2 us (13%)
  matrix products  49.6 us (10%)
  other arithmetic  29.5 us (6%)
  between operations  17.6 us (3%)
  local copies, waits for them, and re-layouts  7.93 us (2%)
    psum x1, waiting for transfers between devices, on_device(): lax.psum(grad_qkv.astype(jnp.bfloat16), 'replica').astype(jnp.float32)  232 us
    reduce_scatter x1, waiting for transfers between devices, on_device(): lax.psum_scatter(grad_qkv_part.astype(jnp.bfloat16), 'group', scatter_dim...  34.2 us
    psum x1, blocking collectives, on_device(): lax.psum(grad_norm1.astype(jnp.bfloat16), 'replica').astype(jnp.float32)  33.8 us
    all_gather x1, waiting for transfers between devices, on_device(): lax.all_gather(out_weight, 'group', axis=0, tiled=True)  23.2 us
    dot_general x5, matrix products, outer_sum(): lax.dot_general(left, right, (((0,), (0,)), ((), ())), preferred_element_...  19.1 us
    reduce_scatter x1, waiting for transfers between devices, on_device(): lax.psum_scatter(matmul(activ_b, down_weight).astype(jnp.bfloat16), 'grou...  16.1 us
    dot_general x5, matrix products, matmul(): return jnp.dot(left, right, preferred_element_type=jnp.float32)  15.2 us
    all_gather x1, waiting for transfers between devices, on_device(): lax.all_gather(qkv_weight, 'group', axis=0, tiled=True)  15 us
  transfers between devices with their start and end apart: 7, of which 7 were waited for; matrix products, arithmetic and copies ran while one was open for 9% of the time, Pallas kernels for 0%

commit v1 on v0

--- a/solution.py
+++ b/solution.py
@@ -221,7 +221,9 @@
     )
     grad_norm1, grad_qkv, grad_bias, grad_out, grad_norm2, grad_gate, grad_up, grad_down = (
         lax.psum(grad_norm1.astype(jnp.bfloat16), "replica").astype(jnp.float32),
-        lax.psum(grad_qkv.astype(jnp.bfloat16), "replica").astype(jnp.float32),
+        jnp.sum(lax.all_gather(grad_qkv.astype(jnp.bfloat16), "replica"), axis=0).astype(
+            jnp.float32
+        ),
         lax.psum(grad_bias.astype(jnp.bfloat16), "replica").astype(jnp.float32),
         lax.psum(grad_out.astype(jnp.bfloat16), "replica").astype(jnp.float32),
         lax.psum(grad_norm2.astype(jnp.bfloat16), "replica").astype(jnp.float32),

time: 506 us -> 610 us (1.21)
  waiting for transfers between devices: 332 us -> 426 us
  other arithmetic: 29.5 us -> 39.7 us
    all_gather x0 -> x1, waiting for transfers between devices: none -> 110 us  [on_device(): lax.all_gather(grad_qkv.astype(jnp.bfloat16), 'replica')]
    psum x1, waiting for transfers between devices: 232 us -> 216 us  [on_device(): lax.psum(grad_out.astype(jnp.bfloat16), 'replica').astype(jnp.float32)]
    reduce_sum x0 -> x1, other arithmetic: none -> 8.84 us  [on_device(): jnp.sum(lax.all_gather(grad_qkv.astype(jnp.bfloat16), 'replica'), axis=0)]
  transfers between devices with their start and end apart: 7 -> 8, of which waited for: 7 -> 8; matrix products, arithmetic and copies ran while one was open for 9% -> 11% of each run, Pallas kernels for 0% -> 0%
where the time goes in v1:
time: 610 us; the launch traced here: 609 us
  waiting for transfers between devices  426 us (70%)
  blocking collectives  68.2 us (11%)
  matrix products  49.6 us (8%)
  other arithmetic  39.7 us (7%)
  between operations  17.5 us (3%)
  local copies, waits for them, and re-layouts  7.88 us (1%)
    psum x1, waiting for transfers between devices, on_device(): lax.psum(grad_out.astype(jnp.bfloat16), 'replica').astype(jnp.float32)  216 us
    all_gather x1, waiting for transfers between devices, on_device(): lax.all_gather(grad_qkv.astype(jnp.bfloat16), 'replica')  110 us
    reduce_scatter x1, waiting for transfers between devices, on_device(): lax.psum_scatter(grad_qkv_part.astype(jnp.bfloat16), 'group', scatter_dim...  34.1 us
    psum x1, blocking collectives, on_device(): lax.psum(grad_norm1.astype(jnp.bfloat16), 'replica').astype(jnp.float32)  33.8 us
    all_gather x1, waiting for transfers between devices, on_device(): lax.all_gather(out_weight, 'group', axis=0, tiled=True)  23.2 us
    dot_general x5, matrix products, outer_sum(): lax.dot_general(left, right, (((0,), (0,)), ((), ())), preferred_element_...  19.1 us
    reduce_scatter x1, waiting for transfers between devices, on_device(): lax.psum_scatter(matmul(activ_b, down_weight).astype(jnp.bfloat16), 'grou...  16.1 us
    dot_general x5, matrix products, matmul(): return jnp.dot(left, right, preferred_element_type=jnp.float32)  15.2 us
  transfers between devices with their start and end apart: 8, of which 8 were waited for; matrix products, arithmetic and copies ran while one was open for 11% of the time, Pallas kernels for 0%

profile of v1, /device:TPU:0, one launch (start us, length us, event | category | flops | bytes accessed | tf_op | source)
XLA Modules:
  0.0 609.2 jit_solution(2737720889557035145)
XLA Ops:
  14.6 5.9 all-reduce.9
  21.0 14.6 %all-gather = bf16[1,288,896]{2,1,0:T(8,128)(2,1)} all-gather(bf16[1,144,896]{2,1,0:T(8,128)(2,1)S(1)} %copy-done.5), channel_id=2, replica_groups=mesh['group'=2,'replica'=16] {'group'}, dimensions={1}, use_global_device_ids=true | all-gather | bytes 774144 | tf_op jit(solution)/shard_map/all_gather | solution.py:136
  35.6 15.0 %all-gather.6.cloned.1.call-done = bf16[896,1152]{1,0:T(8,128)(2,1)} async-done(((bf16[448,1152]{1,0:T(8,128)(2,1)}), bf16[896,1152]{1,0:T(8,128)(2,1)}) %all-gather.6.cloned.1.call-update) | async-done | bytes 2064400 | tf_op jit(solution)/shard_map/all_gather | solution.py:104
  56.6 23.2 %all-gather.8.cloned.1.call-done = bf16[896,896]{1,0:T(8,128)(2,1)} async-done(((bf16[448,896]{1,0:T(8,128)(2,1)}), bf16[896,896]{1,0:T(8,128)(2,1)}) %all-gather.8.cloned.1.call-update) | async-done | bytes 1605648 | tf_op jit(solution)/shard_map/all_gather | solution.py:106
  82.0 8.9 %all_gather.36 = bf16[288,896]{1,0:T(8,128)(2,1)S(1)} all-gather(bf16[144,896]{1,0:T(8,128)(2,1)S(1)} %multiply_convert_fusion.3), channel_id=1, replica_groups=mesh['group'=2,'replica'=16] {'group'}, dimensions={0}, use_global_device_ids=true | all-gather | bytes 774144 | tf_op jit(solution)/shard_map/all_gather | solution.py:135
  90.9 4.1 fusion.53
  96.9 4.0 multiply_convert_fusion
  105.3 5.1 convolution_convert_fusion.5
  110.4 9.4 %reduce-scatter.7.cloned.1.call-done = bf16[144,896]{1,0:T(8,128)(2,1)} async-done(((bf16[288,896]{1,0:T(8,128)(2,1)}), bf16[144,896]{1,0:T(8,128)(2,1)}) %reduce-scatter.7.cloned.1.call-update) | async-done | bytes 258064 | tf_op jit(solution)/shard_map/reduce_scatter | solution.py:155
  121.0 16.1 %reduce-scatter.5.cloned.1.call-done = bf16[144,896]{1,0:T(8,128)(2,1)} async-done(((bf16[288,896]{1,0:T(8,128)(2,1)}), bf16[144,896]{1,0:T(8,128)(2,1)}) %reduce-scatter.5.cloned.1.call-update) | async-done | bytes 258064 | tf_op jit(solution)/shard_map/reduce_scatter | solution.py:143
  139.3 3.0 convolution_convert_fusion.4
  142.6 2.7 convolution_convert_fusion.7
  154.6 4.7 convolution_convert_fusion
  159.3 4.6 convolution_convert_fusion.1
  163.9 4.6 convolution_convert_fusion.2
  169.0 34.1 %reduce-scatter.9.cloned.1.call-done = bf16[448,1152]{1,0:T(8,128)(2,1)} async-done(((bf16[896,1152]{1,0:T(8,128)(2,1)}), bf16[448,1152]{1,0:T(8,128)(2,1)}) %reduce-scatter.9.cloned.1.call-update) | async-done | bytes 1032208 | tf_op jit(solution)/shard_map/reduce_scatter | solution.py:209
  206.1 5.0 all-reduce.8
  211.3 33.8 %all-reduce.6 = (bf16[448]{0:T(512)(128)(2,1)S(1)}, bf16[576]{0:T(1024)(128)(2,1)S(1)}, bf16[448]{0:T(512)(128)(2,1)S(1)}) all-reduce(bf16[448]{0:T(512)(128)(2,1)S(1)} %dynamic-slice.4, bf16[576]{0:T(1024)(128)(2,1)S(1)} %dynamic-slice.6, bf16[448]{0:T(512)(128)(2,1)S(1)} %dynamic-slice.8), channel_id=1, replica_groups=mesh['group'=2,'replica'=16] {'replica'}, use_global_device_ids=true, to_apply=%region_12.13 | all-reduce | flops 1472 | bytes 5888 | tf_op jit(solution)/shard_map/psum | solution.py:223
  248.9 216.0 %all-reduce.12.cloned.1.call-done = (bf16[448,896]{1,0:T(8,128)(2,1)}, bf16[896,2432]{1,0:T(8,128)(2,1)}, bf16[896,2432]{1,0:T(8,128)(2,1)}, bf16[2432,896]{1,0:T(8,128)(2,1)}) async-done(((bf16[448,896]{1,0:T(8,128)(2,1)}, bf16[896,2432]{1,0:T(8,128)(2,1)}, bf16[896,2432]{1,0:T(8,128)(2,1)}, bf16[2432,896]{1,0:T(8,128)(2,1)}), (bf16[448,896]{1,0:T(8,128)(2,1)}, bf16[896,2432]{1,0:T(8,128)(2,1)}, ...) | async-done | bytes 13877264 | tf_op jit(solution)/shard_map/psum | solution.py:228
  467.4 6.4 %convert_element_type.186 = f32[896,2432]{1,0:T(8,128)} convert(bf16[896,2432]{1,0:T(8,128)(2,1)} %get-tuple-element.18) | non-fusion elementwise | flops 2179072 | bytes 13074432 | tf_op jit(solution)/shard_map/convert_element_type | solution.py:230
  473.8 4.1 convert_element_type.188
  477.9 4.1 convert_element_type.190
  482.0 110.1 %all-gather.10.cloned.1.call-done = bf16[7168,1152]{1,0:T(8,128)(2,1)} async-done(((bf16[448,1152]{1,0:T(8,128)(2,1)}), bf16[7168,1152]{1,0:T(8,128)(2,1)}) %all-gather.10.cloned.1.call-update) | async-done | bytes 16515088 | tf_op jit(solution)/shard_map/all_gather | solution.py:224
  592.0 8.8 %reduce_sum.110 = bf16[448,1152]{1,0:T(8,128)(2,1)S(1)} reduce(bf16[16,448,1152]{2,1,0:T(8,128)(2,1)} %bitcast.124, bf16[]{:T(256)} %constant.32.clone.1), dimensions={0}, to_apply=%region_14.15 | reduce | flops 7741440 | bytes 17547266 | tf_op jit(solution)/shard_map/reduce_sum | solution.py:224
  (180 shorter events, 43.3 us)
Async XLA Ops:
  7.2 6.7 %copy-start.26 = (bf16[448]{0:T(512)(128)(2,1)S(1)}, bf16[448]{0:T(512)(128)(2,1)}, u32[]{:S(2)}) copy-start(bf16[448]{0:T(512)(128)(2,1)} %param.13) | copy-start | bytes 2692
  7.2 6.9 %copy-start.27 = (bf16[448]{0:T(512)(128)(2,1)S(1)}, bf16[448]{0:T(512)(128)(2,1)}, u32[]{:S(2)}) copy-start(bf16[448]{0:T(512)(128)(2,1)} %param.17) | copy-start | bytes 2692
  7.2 7.2 %copy-start.25 = (bf16[576]{0:T(1024)(128)(2,1)S(1)}, bf16[576]{0:T(1024)(128)(2,1)}, u32[]{:S(2)}) copy-start(bf16[576]{0:T(1024)(128)(2,1)} %param.15) | copy-start | bytes 3460
  7.2 13.7 %copy-start.5 = (bf16[1,144,896]{2,1,0:T(8,128)(2,1)S(1)}, bf16[1,144,896]{2,1,0:T(8,128)(2,1)}, u32[]{:S(2)}) copy-start(bf16[1,144,896]{2,1,0:T(8,128)(2,1)} %param.21) | copy-start | bytes 774148
  7.2 43.4 %all-gather.6.cloned.1.call-start = ((), (), s32[]{:S(2)}) async-start(), calls=%async_computation.4 | async-start | bytes 3096576 | tf_op jit(solution)/shard_map/all_gather | solution.py:104
  8.0 71.8 %all-gather.8.cloned.1.call-start = ((), (), s32[]{:S(2)}) async-start(), calls=%async_computation.5 | async-start | bytes 2408448 | tf_op jit(solution)/shard_map/all_gather | solution.py:106
  8.7 111.1 %reduce-scatter.7.cloned.1.call-start = ((), (), s32[]{:S(2)}) async-start(), calls=%async_computation.7 | async-start | bytes 774144 | tf_op jit(solution)/shard_map/reduce_scatter | solution.py:155
  20.7 34.3 %copy-start.14 = (f32[144,32]{0,1:T(8,128)}, f32[144,32]{0,1:T(8,128)S(1)}, u32[]{:S(2)}) copy-start(f32[144,32]{0,1:T(8,128)S(1)} %get-tuple-element.43) | copy-start | bytes 55300
  20.9 32.7 %copy-start.10 = (f32[144,32]{1,0:T(8,128)}, f32[144,32]{1,0:T(8,128)S(1)}, u32[]{:S(2)}) copy-start(f32[144,32]{1,0:T(8,128)S(1)} %copy.77) | copy-start | bytes 55300
  21.0 32.6 %copy-start.12 = (f32[144,32]{1,0:T(8,128)}, f32[144,32]{1,0:T(8,128)S(1)}, u32[]{:S(2)}) copy-start(f32[144,32]{1,0:T(8,128)S(1)} %copy.78) | copy-start | bytes 55300
  56.5 34.4 %copy-start.3 = (bf16[2,64,7,144]{3,1,2,0:T(8,128)(2,1)}, bf16[2,64,7,144]{3,1,2,0:T(8,128)(2,1)S(1)}, u32[]{:S(2)}) copy-start(bf16[2,64,7,144]{3,1,2,0:T(8,128)(2,1)S(1)} %convolution_convert_fusion.6) | copy-start | bytes 774148
  82.0 13.1 %slice-start.4 = ((s8[4358144]{0:T(1024)(128)(4,1)}), s8[4194304]{0:T(1024)(128)(4,1)S(1)}, s32[]{:S(2)}) async-start(s8[4358144]{0:T(1024)(128)(4,1)} %bitcast.144), calls=%async_computation.16 | async-start | bytes 8388608
  95.2 7.5 %slice-start.6 = ((s8[4358144]{0:T(1024)(128)(4,1)}), s8[4194304]{0:T(1024)(128)(4,1)S(1)}, s32[]{:S(2)}) async-start(s8[4358144]{0:T(1024)(128)(4,1)} %bitcast.146), calls=%async_computation.18 | async-start | bytes 8388608
  105.2 31.9 %reduce-scatter.5.cloned.1.call-start = ((), (), s32[]{:S(2)}) async-start(), calls=%async_computation.6 | async-start | bytes 774144 | tf_op jit(solution)/shard_map/reduce_scatter | solution.py:143
  110.4 58.5 %reduce-scatter.11.cloned.1.call-start = ((), (), s32[]{:S(2)}) async-start(), calls=%async_computation.9 | async-start | bytes 2408448 | tf_op jit(solution)/shard_map/reduce_scatter | solution.py:215
  142.3 60.8 %reduce-scatter.9.cloned.1.call-start = ((), (), s32[]{:S(2)}) async-start(), calls=%async_computation.8 | async-start | bytes 3096576 | tf_op jit(solution)/shard_map/reduce_scatter | solution.py:209
  154.6 310.3 %all-reduce.12.cloned.1.call-start = ((), (), s32[]{:S(2)}) async-start(), calls=%async_computation.11 | async-start | bytes 27754496 | tf_op jit(solution)/shard_map/psum | solution.py:228
  168.9 35.6 %copy-start.4 = (bf16[896,1152]{1,0:T(8,128)(2,1)S(1)}, bf16[896,1152]{1,0:T(8,128)(2,1)}, u32[]{:S(2)}) copy-start(bf16[896,1152]{1,0:T(8,128)(2,1)} %all-gather.6.cloned.1.call-done) | copy-start | bytes 6193156
  169.0 423.1 %all-gather.10.cloned.1.call-start = ((), (), s32[]{:S(2)}) async-start(), calls=%async_computation.10 | async-start | bytes 17547264 | tf_op jit(solution)/shard_map/all_gather | solution.py:224
  204.4 42.4 %copy-start.1 = (f32[144,896]{1,0:T(8,128)S(1)}, f32[144,896]{1,0:T(8,128)}, u32[]{:S(2)}) copy-start(f32[144,896]{1,0:T(8,128)} %copy-done) | copy-start | bytes 1548292
  204.4 42.4 %copy-start.24 = (f32[144]{0:T(256)S(1)}, f32[144]{0:T(256)}, u32[]{:S(2)}) copy-start(f32[144]{0:T(256)} %get-tuple-element.44) | copy-start | bytes 1732
  464.8 9.0 %slice-start.2 = ((s8[4358144]{0:T(1024)(128)(4,1)}), s8[4194304]{0:T(1024)(128)(4,1)S(1)}, s32[]{:S(2)}) async-start(s8[4358144]{0:T(1024)(128)(4,1)} %bitcast.127), calls=%async_computation.14 | async-start | bytes 8388608
  467.4 6.5 %slice-start.3 = ((s8[4358144]{0:T(1024)(128)(4,1)}), s8[163840]{0:T(1024)(128)(4,1)S(1)}, s32[]{:S(2)}) async-start(s8[4358144]{0:T(1024)(128)(4,1)} %bitcast.127), calls=%async_computation.15 | async-start | bytes 327680
  467.4 10.5 %slice-start = ((s8[4358144]{0:T(1024)(128)(4,1)}), s8[4194304]{0:T(1024)(128)(4,1)S(1)}, s32[]{:S(2)}) async-start(s8[4358144]{0:T(1024)(128)(4,1)} %bitcast.125), calls=%async_computation.12 | async-start | bytes 8388608
  (27 other events, 71.2 us)
Sparse Core Ops, SparseCore 0:
  9.6 40.9 all-gather.5
  52.2 27.5 all-gather.7
  105.3 14.4 reduce-scatter.6
  122.6 14.4 reduce-scatter.4
  142.4 26.4 reduce-scatter.10
  171.6 31.4 reduce-scatter.8
  208.9 255.8 all-reduce.11
  467.1 124.8 all-gather.9
